TPU v7x, 512 devices: a whole 4x8x8 slice. The times are simulated.
512 devices in a mesh: sec: 32 (over z, x), row: 16 (over y, core).
Axes of the slice: x: 4, y: 8, z: 8, core: 2. Of those that a mesh axis runs over, the one named last changes fastest.
Arguments:
- corner_ul: bfloat16 [32, 1024, 1024], P('sec', 'row'), may hold values from -6 to 6
- corner_ur: bfloat16 [32, 1024, 1024], P('sec'), may hold values from -0.1875 to 0.1875
- corner_dl: bfloat16 [32, 1024, 1024], P('sec', 'row'), may hold values from -6 to 6
- corner_dr: bfloat16 [32, 1024, 1024], P('sec'), may hold values from -0.1875 to 0.1875
- left_factor: bfloat16 [32, 1024, 16], P('sec', 'row'), may hold values from -0.1875 to 0.1875
- right_factor: bfloat16 [32, 1024, 16], P('sec', 'row'), may hold values from -0.1875 to 0.1875
- singular: float32 [32, 16], P('sec'), may hold values from 0.25 to 4
- states: int32 [32], P('sec'), may hold values from 8 to 16, as said below
- kept: int32 [32], P('sec'), may hold values from 8 to 16, as said below
- joining_map: int32 [32, 16], P('sec'), may hold values from 0 to 15, each once within a row
Outputs:
- proj_tilde: bfloat16 [32, 1024, 16], P('sec', 'row')
- proj: bfloat16 [32, 1024, 16], P('sec', 'row')
- intersection: float32 [32, 16, 16], P('sec')
Inputs may be any that keep to these rules, and one draw needn't show every extreme that they name: `states`: at least half of 16; some sector has all 16. `kept`: at least half of 16; some sector keeps all 16. `joining_map`: each row is a permutation of 0 to 15.
All inputs are finite; a program needn't handle non-finite values.
Results may differ from a plain program's by a relative error of at most 0.0051.
Values may be sent and summed in bfloat16 or wider, within the bound.
A program may use at most 64 MiB of HBM per device.

v0:
```python
import jax
import jax.numpy as jnp
from jax import lax
from jax.sharding import PartitionSpec as P


def passed_along(value, axis, steps):
    count = lax.axis_size(axis)
    pairs = [(source, (source + steps) % count) for source in range(count)]
    return lax.ppermute(value, axis, pairs)


def local(
    corner_ul,
    corner_ur,
    corner_dl,
    corner_dr,
    left_factor,
    right_factor,
    singular,
    states,
    kept,
    joining_map,
):
    rows_here = corner_ul.shape[1]
    width = corner_ul.shape[2]
    states_here = joining_map.shape[1]
    bonds = width // states_here
    keep_cols = left_factor.shape[2]
    row_count = lax.axis_size("row")
    row_index = lax.axis_index("row")
    positions = row_index * rows_here + jnp.arange(rows_here, dtype=jnp.int32)
    live_rows = (positions % states_here < states[0]).astype(jnp.float32)
    live_cols = (jnp.arange(width, dtype=jnp.int32) % states_here < states[0]).astype(jnp.float32)

    def half(left, right):
        full = jnp.dot(left[0], right[0], preferred_element_type=jnp.float32)
        return (full * live_rows[:, None] * live_cols[None, :]).astype(jnp.bfloat16)

    upper = half(corner_ul, corner_ur)
    lower = half(corner_dl, corner_dr)
    picker = (joining_map[0][:, None] == jnp.arange(states_here, dtype=jnp.int32)[None, :]).astype(
        jnp.bfloat16
    )

    def permute(factor):
        three = factor[0].reshape(rows_here // states_here, states_here, keep_cols)
        moved = jnp.einsum("xz,qxk->qzk", picker, three, preferred_element_type=jnp.float32)
        return moved.astype(jnp.bfloat16).reshape(rows_here, keep_cols)

    u_moved = permute(left_factor)
    v_moved = permute(right_factor)
    up_in = passed_along(upper, "sec", 1)
    low_in = passed_along(lower, "sec", -1)
    swapped_up, swapped_low = (
        lax.all_to_all(up_in, "row", split_axis=1, concat_axis=0, tiled=True),
        lax.all_to_all(low_in, "row", split_axis=1, concat_axis=0, tiled=True),
    )
    local_bonds = bonds // row_count

    def one(swapped, factor):
        block4 = swapped.reshape(bonds, states_here, local_bonds, states_here)
        factor3 = factor.reshape(local_bonds, states_here, keep_cols)
        result = jnp.einsum("pzqy,qzk->pyk", block4, factor3, preferred_element_type=jnp.float32)
        return result.reshape(lax.axis_size("row") * rows_here, keep_cols)

    summed = lax.psum_scatter(
        jnp.concatenate([one(swapped_up, u_moved), one(swapped_low, v_moved)], axis=1),
        "row",
        scatter_dimension=0,
        tiled=True,
    )
    a_part = summed[:, :keep_cols]
    b_part = summed[:, keep_cols:]
    columns = jnp.arange(keep_cols, dtype=jnp.int32)
    weight = jnp.where(columns < kept[0], 1.0 / jnp.sqrt(singular[0]), 0.0)
    scaled_a = a_part * weight[None, :]
    scaled_b = b_part * weight[None, :]
    partial_intersection = jnp.dot(
        scaled_a.T, scaled_b, precision=lax.Precision.HIGHEST, preferred_element_type=jnp.float32
    )
    intersection = lax.psum(partial_intersection, "row") / jnp.sqrt(jnp.float32(width))
    return (
        scaled_a.astype(jnp.bfloat16)[None],
        scaled_b.astype(jnp.bfloat16)[None],
        intersection[None],
    )


def solution(mesh):
    placed = (
        P("sec", "row", None),
        P("sec", None, None),
        P("sec", "row", None),
        P("sec", None, None),
        P("sec", "row", None),
        P("sec", "row", None),
        P("sec", None),
        P("sec"),
        P("sec"),
        P("sec", None),
    )
    return jax.shard_map(
        local,
        mesh=mesh,
        in_specs=placed,
        out_specs=(P("sec", "row", None), P("sec", "row", None), P("sec", None, None)),
        check_vma=False,
    )
```

profile of v0, /device:TPU:1, one launch (start us, length us, event | category | flops | bytes accessed | tf_op | source)
XLA Modules:
  0.0 161.8 jit_solution(4474918008841112269)
XLA Ops:
  7.2 0.0 copy-start
  7.2 0.0 copy-start.2
  8.0 0.8 copy-done
  8.8 1.4 fusion.19
  10.2 3.9 %collective-permute-start = (bf16[64,1024]{1,0:T(8,128)(2,1)S(1)}, bf16[64,1024]{1,0:T(8,128)(2,1)S(1)}, u32[]{:S(2)}, u32[]{:S(2)}) collective-permute-start(bf16[64,1024]{1,0:T(8,128)(2,1)S(1)} %fusion.19), channel_id=1, source_target_pairs={{0,16},{16,32},{32,48},{48,64},{64,80},{80,96},{96,112},{112,128},... | collective-permute-start | bytes 393224 | tf_op jit(solution)/shard_map/ppermute | solution.py:10
  14.1 12.9 %collective-permute-done = bf16[64,1024]{1,0:T(8,128)(2,1)S(1)} collective-permute-done((bf16[64,1024]{1,0:T(8,128)(2,1)S(1)}, bf16[64,1024]{1,0:T(8,128)(2,1)S(1)}, u32[]{:S(2)}, u32[]{:S(2)}) %collective-permute-start) | collective-permute-done | bytes 131104 | tf_op jit(solution)/shard_map/ppermute | solution.py:10
  27.0 0.2 copy.29
  27.2 0.0 copy-start.4
  27.2 0.0 copy-start.5
  27.2 0.9 reshape.69
  28.1 8.4 %all-to-all-start = ((bf16[16,2,2048]{2,1,0:T(2,128)(2,1)}), bf16[16,2,2048]{2,1,0:T(2,128)(2,1)S(1)}, u32[]{:S(2)}, u32[]{:S(2)}) async-start(bf16[16,2,2048]{2,1,0:T(2,128)(2,1)} %reshape.69), calls=%async_computation | async-start | bytes 262144 | tf_op jit(solution)/shard_map/all_to_all | solution.py:56
  36.5 0.0 copy-done.2
  36.5 2.1 %fusion.16 = bf16[64,1024]{1,0:T(8,128)(2,1)S(1)} fusion(bf16[1,1024,1024]{2,1,0:T(8,128)(2,1)} %param.13, bf16[1,64,1024]{2,1,0:T(8,128)(2,1)S(1)} %copy-done.2, f32[1024]{0:T(1024)S(1)} %fusion.45, f32[64]{0:T(128)S(1)} %compare_convert_fusion), kind=kOutput, calls=%fused_computation.8 | convolution fusion | flops 134414336 | bytes 2363648 | tf_op jit(solution)/shard_map/dot_general | solution.py:37
  38.6 3.4 %collective-permute-start.1 = (bf16[64,1024]{1,0:T(8,128)(2,1)S(1)}, bf16[64,1024]{1,0:T(8,128)(2,1)S(1)}, u32[]{:S(2)}, u32[]{:S(2)}) collective-permute-start(bf16[64,1024]{1,0:T(8,128)(2,1)S(1)} %fusion.16), channel_id=1, source_target_pairs={{0,496},{16,0},{32,16},{48,32},{64,48},{80,64},{96,80},{112,96},{1... | collective-permute-start | bytes 393224 | tf_op jit(solution)/shard_map/ppermute | solution.py:10
  42.0 3.5 %collective-permute-done.1 = bf16[64,1024]{1,0:T(8,128)(2,1)S(1)} collective-permute-done((bf16[64,1024]{1,0:T(8,128)(2,1)S(1)}, bf16[64,1024]{1,0:T(8,128)(2,1)S(1)}, u32[]{:S(2)}, u32[]{:S(2)}) %collective-permute-start.1) | collective-permute-done | bytes 131104 | tf_op jit(solution)/shard_map/ppermute | solution.py:10
  45.4 0.2 copy.31
  45.6 0.9 reshape.67
  46.5 0.0 all-to-all-done
  46.5 7.8 %all-to-all-start.1 = ((bf16[16,2,2048]{2,1,0:T(2,128)(2,1)}), bf16[16,2,2048]{2,1,0:T(2,128)(2,1)S(1)}, u32[]{:S(2)}, u32[]{:S(2)}) async-start(bf16[16,2,2048]{2,1,0:T(2,128)(2,1)} %reshape.67), calls=%async_computation.1 | async-start | bytes 262144 | tf_op jit(solution)/shard_map/all_to_all | solution.py:57
  54.3 0.0 reduce-scatter.4.cloned.1.call-start
  54.3 0.0 copy-done.4
  54.4 0.7 copy.30
  55.0 0.0 copy-done.5
  55.0 0.1 copy.32
  55.1 0.2 reshape.70
  55.4 0.2 copy.18
  55.6 0.4 reshape.60
  56.0 2.9 %copy.19 = bf16[64,16,4,16]{1,0,3,2:T(8,128)(2,1)} copy(bf16[64,16,4,16]{3,0,1,2:T(8,128)(2,1)S(1)} %bitcast.89) | data formatting | bytes 262144 | tf_op jit(solution)/shard_map/pzqy,qzk->pyk/dot_general | solution.py:64
  58.9 3.6 %dot_general.31 = bf16[1024,4,16]{0,2,1:T(8,128)(2,1)} reshape(bf16[64,16,4,16]{1,0,3,2:T(8,128)(2,1)} %copy.19) | data formatting | bytes 262144 | tf_op jit(solution)/shard_map/pzqy,qzk->pyk/dot_general | solution.py:64
  62.5 0.7 all-to-all-done.1
  63.2 0.2 reshape.68
  63.4 0.2 copy.23
  63.6 0.0 copy-start.1
  63.6 0.4 reshape.61
  64.0 0.0 copy-start.3
  64.0 0.0 copy-start.6
  64.1 0.0 copy-start.7
  64.1 2.9 %copy.24 = bf16[64,16,4,16]{1,0,3,2:T(8,128)(2,1)} copy(bf16[64,16,4,16]{3,0,1,2:T(8,128)(2,1)S(1)} %bitcast.90) | data formatting | bytes 262144 | tf_op jit(solution)/shard_map/pzqy,qzk->pyk/dot_general | solution.py:64
  66.9 3.0 %dot_general.36 = bf16[1024,4,16]{0,2,1:T(8,128)(2,1)S(1)} reshape(bf16[64,16,4,16]{1,0,3,2:T(8,128)(2,1)} %copy.24) | data formatting | bytes 262144 | tf_op jit(solution)/shard_map/pzqy,qzk->pyk/dot_general | solution.py:64
  69.9 0.0 copy-done.1
  69.9 0.0 copy-done.3
  69.9 0.0 copy-done.6
  69.9 0.3 convolution_bitcast_fusion.1
  70.2 0.3 convolution_bitcast_fusion
  70.5 1.0 copy.33
  71.5 0.0 reduce-scatter.4.cloned.1.call-update
  72.2 0.0 copy-done.7
  72.2 54.5 %reduce-scatter.4.cloned.1.call-done = f32[64,32]{1,0:T(8,128)} async-done(((f32[1024,32]{1,0:T(8,128)}), f32[64,32]{1,0:T(8,128)}) %reduce-scatter.4.cloned.1.call-update) | async-done | bytes 8208
  126.8 0.9 fusion.48
  127.7 0.1 copy.35
  127.8 0.1 copy.36
  127.8 0.7 fusion.36
  128.5 0.2 fusion.31
  128.7 25.6 %psum.7 = f32[16,16]{1,0:T(8,128)S(1)} all-reduce(f32[16,16]{1,0:T(8,128)S(1)} %fusion.31), channel_id=1, replica_groups=mesh['sec'=32,'row'=16] {'row'}, use_global_device_ids=true, to_apply=%region_1.2 | all-reduce | flops 256 | bytes 2048 | tf_op jit(solution)/shard_map/psum | solution.py:82
  154.3 0.6 multiply_bitcast_fusion
  (6 shorter events, 0.1 us)
Async XLA Ops:
  7.2 1.6 copy-start
  7.2 29.3 %copy-start.2 = (bf16[1,64,1024]{2,1,0:T(8,128)(2,1)S(1)}, bf16[1,64,1024]{2,1,0:T(8,128)(2,1)}, u32[]{:S(2)}) copy-start(bf16[1,64,1024]{2,1,0:T(8,128)(2,1)} %param.12) | copy-start | bytes 393220
  10.2 16.9 %collective-permute-start = (bf16[64,1024]{1,0:T(8,128)(2,1)S(1)}, bf16[64,1024]{1,0:T(8,128)(2,1)S(1)}, u32[]{:S(2)}, u32[]{:S(2)}) collective-permute-start(bf16[64,1024]{1,0:T(8,128)(2,1)S(1)} %fusion.19), channel_id=1, source_target_pairs={{0,16},{16,32},{32,48},{48,64},{64,80},{80,96},{96,112},{112,128},... | collective-permute-start | bytes 393224 | tf_op jit(solution)/shard_map/ppermute | solution.py:10
  27.2 27.1 %copy-start.4 = (bf16[1,64,16]{1,2,0:T(8,128)(2,1)S(1)}, bf16[1,64,16]{1,2,0:T(8,128)(2,1)}, u32[]{:S(2)}) copy-start(bf16[1,64,16]{1,2,0:T(8,128)(2,1)} %param.14) | copy-start | bytes 6148
  27.2 27.8 %copy-start.5 = (bf16[1,64,16]{1,2,0:T(8,128)(2,1)S(1)}, bf16[1,64,16]{1,2,0:T(8,128)(2,1)}, u32[]{:S(2)}) copy-start(bf16[1,64,16]{1,2,0:T(8,128)(2,1)} %param.15) | copy-start | bytes 6148
  28.1 18.4 %all-to-all-start = ((bf16[16,2,2048]{2,1,0:T(2,128)(2,1)}), bf16[16,2,2048]{2,1,0:T(2,128)(2,1)S(1)}, u32[]{:S(2)}, u32[]{:S(2)}) async-start(bf16[16,2,2048]{2,1,0:T(2,128)(2,1)} %reshape.69), calls=%async_computation | async-start | bytes 262144 | tf_op jit(solution)/shard_map/all_to_all | solution.py:56
  38.6 6.8 %collective-permute-start.1 = (bf16[64,1024]{1,0:T(8,128)(2,1)S(1)}, bf16[64,1024]{1,0:T(8,128)(2,1)S(1)}, u32[]{:S(2)}, u32[]{:S(2)}) collective-permute-start(bf16[64,1024]{1,0:T(8,128)(2,1)S(1)} %fusion.16), channel_id=1, source_target_pairs={{0,496},{16,0},{32,16},{48,32},{64,48},{80,64},{96,80},{112,96},{1... | collective-permute-start | bytes 393224 | tf_op jit(solution)/shard_map/ppermute | solution.py:10
  46.5 16.7 %all-to-all-start.1 = ((bf16[16,2,2048]{2,1,0:T(2,128)(2,1)}), bf16[16,2,2048]{2,1,0:T(2,128)(2,1)S(1)}, u32[]{:S(2)}, u32[]{:S(2)}) async-start(bf16[16,2,2048]{2,1,0:T(2,128)(2,1)} %reshape.67), calls=%async_computation.1 | async-start | bytes 262144 | tf_op jit(solution)/shard_map/all_to_all | solution.py:57
  54.3 72.5 %reduce-scatter.4.cloned.1.call-start = ((), (), s32[]{:S(2)}) async-start(), calls=%async_computation.3 | async-start | bytes 557056
  63.6 6.3 %copy-start.1 = (bf16[1024,4,16]{0,2,1:T(8,128)(2,1)S(1)}, bf16[1024,4,16]{0,2,1:T(8,128)(2,1)}, u32[]{:S(2)}) copy-start(bf16[1024,4,16]{0,2,1:T(8,128)(2,1)} %dot_general.31) | copy-start | bytes 393220
  64.0 5.9 %copy-start.3 = (bf16[1,64,16]{2,1,0:T(8,128)(2,1)S(1)}, bf16[1,64,16]{2,1,0:T(8,128)(2,1)}, u32[]{:S(2)}) copy-start(bf16[1,64,16]{2,1,0:T(8,128)(2,1)} %copy.30) | copy-start | bytes 6148
  64.0 5.9 %copy-start.6 = (s32[1,16]{1,0:T(1,128)S(1)}, s32[1,16]{1,0:T(1,128)}, u32[]{:S(2)}) copy-start(s32[1,16]{1,0:T(1,128)} %param.19) | copy-start | bytes 196
  64.1 8.2 %copy-start.7 = (f32[1,16]{1,0:T(1,128)S(1)}, f32[1,16]{1,0:T(1,128)}, u32[]{:S(2)}) copy-start(f32[1,16]{1,0:T(1,128)} %param.16) | copy-start | bytes 196
Sparse Core Ops, SparseCore 0:
  71.7 55.0 reduce-scatter.3
where the time goes:
time: 162 us
  waiting for transfers between devices  71.7 us (44%)
  blocking collectives  25.6 us (16%)
  starting transfers between devices  23.5 us (15%)
  local copies, waits for them, and re-layouts  19.6 us (12%)
  between operations  15.7 us (10%)
  matrix products  4.25 us (3%)
    unnamed x2, waiting for transfers between devices  54.6 us
    psum x1, blocking collectives, local(): lax.psum(partial_intersection, 'row') / jnp.sqrt(jnp.float32(width))  25.6 us
    ppermute x2, waiting for transfers between devices, passed_along(): return lax.ppermute(value, axis, pairs)  16.4 us
    dot_general x4, local copies, waits for them, and re-layouts, one(): jnp.einsum('pzqy,qzk->pyk', block4, factor3, preferred_element_type=jnp.f...  12.3 us
    all_to_all x1, starting transfers between devices, local(): lax.all_to_all(up_in, 'row', split_axis=1, concat_axis=0, tiled=True)  8.36 us
    all_to_all x1, starting transfers between devices, local(): lax.all_to_all(low_in, 'row', split_axis=1, concat_axis=0, tiled=True)  7.8 us
    ppermute x2, starting transfers between devices, passed_along(): return lax.ppermute(value, axis, pairs)  7.3 us
    unnamed x23, local copies, waits for them, and re-layouts  4.13 us
  transfers between devices with their start and end apart: 5, of which 4 were waited for; matrix products, arithmetic and copies ran while one was open for 7% of the time, Pallas kernels for 0%

commit v1 on v0

v1 whole, which is shorter than its diff:
```python
import functools

import jax
import jax.numpy as jnp
from jax import lax
from jax.experimental import pallas as pl
from jax.experimental.pallas import tpu as pltpu
from jax.sharding import PartitionSpec as P

MESH = pl.DeviceIdType.MESH
F32 = jnp.float32
BF16 = jnp.bfloat16
LANES = 128
NT = (((1,), (1,)), ((), ()))


def kernel(
    n_sec, n_row,
    ul, ur, dl, dr, lf, rf, sg, st, kp, jm,
    pt, pj, it,
    v_left, v_right, v_fac, v_sg, v_jm, s_st, s_kp,
    gathered, outgoing, incoming, partial,
    big_sem, small_sem, g_send, g_recv, h_send, h_recv, i_send, i_recv,
):
    rows, width = ul.shape
    ks = lf.shape[0]
    chs = jm.shape[1]
    tiles = width // LANES
    chunk = 2 * LANES
    chunks = width // chunk
    sec = lax.axis_index("sec")
    row = lax.axis_index("row")
    near = (lax.rem(sec + 1, n_sec), lax.rem(sec + n_sec - 1, n_sec))
    y, core = row // 2, lax.rem(row, 2)
    n_y = n_row // 2
    steps = sorted(range(1, n_y), key=lambda d: -min(d, n_y - d))
    peers = [lax.rem(y + d, n_y) * 2 + c for d in steps for c in range(2)] + [y * 2 + 1 - core]

    lefts, rights = (ul, dl), (ur, dr)
    small = [
        pltpu.make_async_copy(lf, v_fac.at[pl.ds(0, ks)], small_sem.at[0]),
        pltpu.make_async_copy(rf, v_fac.at[pl.ds(ks, ks)], small_sem.at[1]),
        pltpu.make_async_copy(jm, v_jm, small_sem.at[2]),
        pltpu.make_async_copy(st, s_st, small_sem.at[3]),
        pltpu.make_async_copy(sg, v_sg, small_sem.at[4]),
        pltpu.make_async_copy(kp, s_kp, small_sem.at[5]),
    ]
    left_in = [pltpu.make_async_copy(lefts[h], v_left.at[h], small_sem.at[6 + h]) for h in range(2)]
    right_in = [
        [
            pltpu.make_async_copy(
                rights[h].at[:, pl.ds(c * chunk, chunk)],
                v_right.at[h, :, pl.ds(c * chunk, chunk)],
                big_sem.at[h, c],
            )
            for c in range(chunks)
        ]
        for h in range(2)
    ]
    for copy in small:
        copy.start()
    for h in range(2):
        left_in[h].start()
    for c in range(chunks):
        for h in range(2):
            right_in[h][c].start()

    barrier = pltpu.get_barrier_semaphore()
    for peer in peers:
        pl.semaphore_signal(barrier, inc=1, device_id={"row": peer}, device_id_type=MESH)
    for other in near:
        pl.semaphore_signal(barrier, inc=1, device_id={"sec": other}, device_id_type=MESH)

    for copy in small:
        copy.wait()

    seq = jnp.concatenate([v_jm[...]] * (rows // chs), axis=1)
    r64 = lax.broadcasted_iota(jnp.int32, (rows, rows), 0)
    c64 = lax.broadcasted_iota(jnp.int32, (rows, rows), 1)
    picker = jnp.where((r64 // chs == c64 // chs) & (lax.rem(r64, chs) == seq), 1.0, 0.0).astype(BF16)
    moved = lax.dot_general(v_fac[...], picker, NT, preferred_element_type=F32)
    gathered[row] = moved.astype(BF16)

    k_row = lax.broadcasted_iota(jnp.int32, (1, ks), 1)
    w_row = jnp.where(k_row < s_kp[0], 1.0 / jnp.sqrt(v_sg[...]), 0.0)
    rk = lax.broadcasted_iota(jnp.int32, (ks, ks), 0)
    ck = lax.broadcasted_iota(jnp.int32, (ks, ks), 1)
    weight = jnp.sum(jnp.where(rk == ck, jnp.broadcast_to(w_row, (ks, ks)), 0.0), axis=1, keepdims=True)

    states = s_st[0]
    lane = lax.broadcasted_iota(jnp.int32, (rows, LANES), 1)
    sub = lax.broadcasted_iota(jnp.int32, (rows, LANES), 0)
    live = (lax.rem(lane, chs) < states) & (lax.rem(sub, chs) < states)
    lane1 = lax.broadcasted_iota(jnp.int32, (2 * chs, LANES), 1)
    low2 = lax.rem(lane1 // (2 * chs), 2) == 0
    lane0 = lax.broadcasted_iota(jnp.int32, (chs, LANES), 1)
    low1 = lax.rem(lane0 // chs, 2) == 0

    def swap_blocks(tile):
        a, b = tile[: 2 * chs], tile[2 * chs :]
        ab = (
            jnp.where(low2, a, pltpu.roll(b, 2 * chs, 1)),
            jnp.where(low2, pltpu.roll(a, LANES - 2 * chs, 1), b),
        )
        out = []
        for half in ab:
            a, b = half[:chs], half[chs:]
            out.append(jnp.where(low1, a, pltpu.roll(b, chs, 1)))
            out.append(jnp.where(low1, pltpu.roll(a, LANES - chs, 1), b))
        return jnp.concatenate(out, axis=0)

    def half_copy(h, c):
        return pltpu.make_async_remote_copy(
            src_ref=outgoing.at[h, pl.ds(2 * c, 2)],
            dst_ref=incoming.at[h, pl.ds(2 * c, 2)],
            send_sem=h_send.at[h, c],
            recv_sem=h_recv.at[h, c],
            device_id={"sec": near[h]},
            device_id_type=MESH,
        )

    def compute(h, c):
        right_in[h][c].wait()
        full = jnp.dot(
            v_left[h], v_right[h, :, pl.ds(c * chunk, chunk)], preferred_element_type=F32
        )
        for i in range(2):
            tile = jnp.where(live, full[:, i * LANES : (i + 1) * LANES], 0.0)
            outgoing[h, 2 * c + i] = swap_blocks(tile).astype(BF16)

    for h in range(2):
        left_in[h].wait()
    for c in range(chunks):
        for h in range(2):
            compute(h, c)

    pl.semaphore_wait(barrier, n_row - 1 + 2)

    def gather_copy(slot, peer):
        return pltpu.make_async_remote_copy(
            src_ref=gathered.at[slot],
            dst_ref=gathered.at[slot],
            send_sem=g_send.at[peer],
            recv_sem=g_recv.at[slot],
            device_id={"row": peer},
            device_id_type=MESH,
        )

    for peer in peers:
        gather_copy(row, peer).start()
    for c in range(chunks):
        for h in range(2):
            half_copy(h, c).start()

    for peer in peers:
        gather_copy(peer, peer).wait_recv()

    halves = []
    for h in range(2):
        total = jnp.zeros((2 * ks, LANES), F32)
        for c in range(chunks):
            half_copy(h, c).wait_recv()
            for t in (2 * c, 2 * c + 1):
                lhs = jnp.concatenate(
                    [gathered[2 * t, pl.ds(h * ks, ks)], gathered[2 * t + 1, pl.ds(h * ks, ks)]], axis=0
                )
                total = total + jnp.dot(lhs, incoming[h, t], preferred_element_type=F32)
        halves.append((total[:ks, :rows] + total[ks:, rows:]) * weight)
    scaled_a, scaled_b = halves
    pt[...] = scaled_a.astype(BF16)
    pj[...] = scaled_b.astype(BF16)

    groups = LANES // ks
    wide = lax.dot_general(
        scaled_a,
        jnp.concatenate([scaled_b] * groups, axis=0),
        NT,
        precision=lax.Precision.HIGHEST,
        preferred_element_type=F32,
    )
    rw = lax.broadcasted_iota(jnp.int32, (ks, LANES), 0)
    cw = lax.broadcasted_iota(jnp.int32, (ks, LANES), 1)
    own = lax.rem(rw, groups) == cw // ks
    wide = jnp.where(own, wide, 0.0)
    for i in range(ks // groups):
        partial[row, pl.ds(i, 1)] = jnp.sum(wide[i * groups : (i + 1) * groups], axis=0, keepdims=True)

    def partial_copy(slot, peer):
        return pltpu.make_async_remote_copy(
            src_ref=partial.at[slot],
            dst_ref=partial.at[slot],
            send_sem=i_send.at[peer],
            recv_sem=i_recv.at[slot],
            device_id={"row": peer},
            device_id_type=MESH,
        )

    for peer in peers:
        partial_copy(row, peer).start()
    for peer in peers:
        gather_copy(row, peer).wait_send()
    for c in range(chunks):
        for h in range(2):
            half_copy(h, c).wait_send()
    for peer in peers:
        partial_copy(peer, peer).wait_recv()
    summed = partial[0]
    for i in range(1, n_row):
        summed = summed + partial[i]
    spread = jnp.concatenate(
        [jnp.broadcast_to(summed[i : i + 1], (groups, LANES)) for i in range(ks // groups)], axis=0
    )
    spread = jnp.where(own, spread, 0.0)
    shift = LANES // 2
    while shift >= ks:
        spread = spread + pltpu.roll(spread, shift, 1)
        shift //= 2
    it[...] = spread[:, :ks] / jnp.sqrt(F32(width))
    for peer in peers:
        partial_copy(row, peer).wait_send()


def local(
    corner_ul, corner_ur, corner_dl, corner_dr, left_factor, right_factor, singular, states, kept, joining_map
):
    n_sec, n_row = lax.axis_size("sec"), lax.axis_size("row")
    rows, width = corner_ul.shape[1:]
    ks = left_factor.shape[2]
    chs = joining_map.shape[1]
    tiles = width // LANES
    dma = pltpu.SemaphoreType.DMA
    pt, pj, it = pl.pallas_call(
        functools.partial(kernel, n_sec, n_row),
        out_shape=(
            jax.ShapeDtypeStruct((ks, rows), BF16),
            jax.ShapeDtypeStruct((ks, rows), BF16),
            jax.ShapeDtypeStruct((ks, ks), F32),
        ),
        in_specs=[pl.BlockSpec(memory_space=pl.ANY)] * 10,
        out_specs=(pl.BlockSpec(memory_space=pltpu.VMEM),) * 3,
        scratch_shapes=[
            pltpu.VMEM((2, rows, width), BF16),
            pltpu.VMEM((2, width, width), BF16),
            pltpu.VMEM((2 * ks, rows), BF16),
            pltpu.VMEM((1, ks), F32),
            pltpu.VMEM((1, chs), jnp.int32),
            pltpu.SMEM((1,), jnp.int32),
            pltpu.SMEM((1,), jnp.int32),
            pltpu.VMEM((n_row, 2 * ks, rows), BF16),
            pltpu.VMEM((2, tiles, rows, LANES), BF16),
            pltpu.VMEM((2, tiles, rows, LANES), BF16),
            pltpu.VMEM((n_row, ks * ks // LANES, LANES), F32),
            dma((2, 4)),
            dma((8,)),
            dma((n_row,)),
            dma((n_row,)),
            dma((2, 4)),
            dma((2, 4)),
            dma((n_row,)),
            dma((n_row,)),
        ],
        compiler_params=pltpu.CompilerParams(collective_id=0, has_side_effects=True),
    )(
        corner_ul[0], corner_ur[0], corner_dl[0], corner_dr[0],
        left_factor[0].T, right_factor[0].T,
        singular, states, kept, joining_map,
    )
    return pt.T[None], pj.T[None], it[None]


def solution(mesh):
    placed = (
        P("sec", "row", None),
        P("sec", None, None),
        P("sec", "row", None),
        P("sec", None, None),
        P("sec", "row", None),
        P("sec", "row", None),
        P("sec", None),
        P("sec"),
        P("sec"),
        P("sec", None),
    )
    return jax.shard_map(
        local,
        mesh=mesh,
        in_specs=placed,
        out_specs=(P("sec", "row", None), P("sec", "row", None), P("sec", None, None)),
        check_vma=False,
    )
```

time: 162 us -> 38.1 us (0.24)
  waiting for transfers between devices: 71.7 us -> 0 us
  Pallas kernels: 0 us -> 32.1 us
  blocking collectives: 25.6 us -> 0 us
  starting transfers between devices: 23.5 us -> 0 us
  local copies, waits for them, and re-layouts: 19.6 us -> 3.83 us
  between operations: 15.7 us -> 1.93 us
  matrix products: 4.25 us -> 0 us
    unnamed x2 -> x0, waiting for transfers between devices: 54.6 us -> none
    pallas_call x0 -> x1, Pallas kernels: none -> 32.1 us  [local(): pl.pallas_call(functools.partial(kernel, n_sec, n_row), out_shape=(jax.Sh...]
    psum x1 -> x0, blocking collectives: 25.6 us -> none  [local(): lax.psum(partial_intersection, 'row') / jnp.sqrt(jnp.float32(width))]
    ppermute x2 -> x0, waiting for transfers between devices: 16.4 us -> none  [passed_along(): return lax.ppermute(value, axis, pairs)]
    all_to_all x2 -> x0, starting transfers between devices: 16.2 us -> none  [the longest x1 8.36 us: local(): lax.all_to_all(up_in, 'row', split_axis=1, concat_axis=0, tiled=True)]
    dot_general x4 -> x0, local copies, waits for them, and re-layouts: 12.3 us -> none  [one(): jnp.einsum('pzqy,qzk->pyk', block4, factor3, preferred_element_type=jnp.f...]
    ppermute x2 -> x0, starting transfers between devices: 7.3 us -> none  [passed_along(): return lax.ppermute(value, axis, pairs)]
    dot_general x5 -> x0, matrix products: 4.25 us -> none  [the longest x2 3.46 us: half(): full = jnp.dot(left[0], right[0], preferred_element_type=jnp.float32)]
  transfers between devices with their start and end apart: 5 -> 0, of which waited for: 4 -> 0; matrix products, arithmetic and copies ran while one was open for 7% -> 0% of each run, Pallas kernels for 0% -> 0%
where the time goes in v1:
time: 38.1 us; the launch traced here: 37.8 us
  Pallas kernels  32.1 us (84%)
  local copies, waits for them, and re-layouts  3.83 us (10%)
  between operations  1.93 us (5%)
    pallas_call x1, Pallas kernels, local(): pl.pallas_call(functools.partial(kernel, n_sec, n_row), out_shape=(jax.Sh...  32.1 us
    unnamed x3, local copies, waits for them, and re-layouts  3.83 us

profile of v1, /device:TPU:1, one launch (start us, length us, event | category | flops | bytes accessed | tf_op | source)
XLA Modules:
  0.0 37.8 jit_solution(12290409635548185241)
XLA Ops:
  1.9 32.1 %shard_map.121 = (bf16[16,64]{1,0:T(8,128)(2,1)}, bf16[16,64]{1,0:T(8,128)(2,1)}, f32[16,16]{1,0:T(8,128)}) custom-call(bf16[64,1024]{1,0:T(8,128)(2,1)} %bitcast.19, bf16[1024,1024]{1,0:T(8,128)(2,1)} %bitcast.17, bf16[64,1024]{1,0:T(8,128)(2,1)} %bitcast.20, bf16[1024,1024]{1,0:T(8,128)(2,1)} %bitcast.18, bf16[16,64]{1,0:T(8,128)(2,1)} %bitcast.24, ...), custom_call_target="tpu_custom_call" | custom-call | tf_op jit(solution)/shard_map/pallas_call | solution.py:232
  34.0 1.3 %copy.18 = bf16[1,64,16]{1,2,0:T(8,128)(2,1)} copy(bf16[1,64,16]{1,2,0:T(8,128)(2,1)} %bitcast.23) | data formatting | bytes 4096
  35.3 1.3 %copy.19 = bf16[1,64,16]{1,2,0:T(8,128)(2,1)} copy(bf16[1,64,16]{1,2,0:T(8,128)(2,1)} %bitcast.22) | data formatting | bytes 4096
  36.5 1.3 %copy.20 = f32[1,16,16]{2,1,0:T(8,128)} copy(f32[1,16,16]{2,1,0:T(8,128)} %bitcast.21) | data formatting | bytes 2048

commit v2 on v1

v2 whole, which is shorter than its diff:
```python
import functools

import jax
import jax.numpy as jnp
from jax import lax
from jax.experimental import pallas as pl
from jax.experimental.pallas import tpu as pltpu
from jax.sharding import PartitionSpec as P

MESH = pl.DeviceIdType.MESH
F32 = jnp.float32
BF16 = jnp.bfloat16
LANES = 128
NT = (((1,), (1,)), ((), ()))


def kernel(
    n_sec, n_row,
    ul, ur, dl, dr, lf, rf, sg, st, kp, jm,
    pt, pj, it,
    v_left, v_right, v_fac, v_sg, v_jm,
    gathered, outgoing, incoming, partial,
    big_sem, small_sem, g_send, g_recv, h_send, h_recv, i_send, i_recv,
):
    rows, width = ul.shape
    ks = lf.shape[0]
    chs = jm.shape[1]
    chunk = 2 * LANES
    chunks = width // chunk
    sec = lax.axis_index("sec")
    row = lax.axis_index("row")
    near = (lax.rem(sec + 1, n_sec), lax.rem(sec + n_sec - 1, n_sec))
    offsets = sorted(range(1, n_row), key=lambda d: -min(d, n_row - d))

    def peer(offset):
        return lax.rem(row + offset, n_row)

    lefts, rights = (ul, dl), (ur, dr)
    left_in = [pltpu.make_async_copy(lefts[h], v_left.at[h], small_sem.at[4 + h]) for h in range(2)]
    right_in = [
        [
            pltpu.make_async_copy(
                rights[h].at[:, pl.ds(c * chunk, chunk)],
                v_right.at[h, :, pl.ds(c * chunk, chunk)],
                big_sem.at[h, c],
            )
            for c in range(chunks)
        ]
        for h in range(2)
    ]
    small = [
        pltpu.make_async_copy(lf, v_fac.at[0], small_sem.at[0]),
        pltpu.make_async_copy(rf, v_fac.at[1], small_sem.at[1]),
        pltpu.make_async_copy(jm, v_jm, small_sem.at[2]),
        pltpu.make_async_copy(sg, v_sg, small_sem.at[3]),
    ]
    for copy in small:
        copy.start()
    for h in range(2):
        left_in[h].start()
    for c in range(chunks):
        for h in range(2):
            right_in[h][c].start()

    barrier = pltpu.get_barrier_semaphore()
    for other in near:
        pl.semaphore_signal(barrier, inc=1, device_id={"sec": other}, device_id_type=MESH)
    for offset in offsets:
        pl.semaphore_signal(barrier, inc=1, device_id={"row": peer(offset)}, device_id_type=MESH)

    def iota(shape, axis):
        return lax.broadcasted_iota(jnp.int32, shape, axis)

    r_pick, c_pick = iota((2 * rows, rows), 0), iota((2 * rows, rows), 1)
    same = lax.rem(r_pick, rows) // chs == c_pick // chs
    z_pick = lax.rem(r_pick, chs)
    left_rows = r_pick < rows
    states = st[0]
    lane, sub = iota((rows, LANES), 1), iota((rows, LANES), 0)
    live = (lax.rem(lane, chs) < states) & (lax.rem(sub, chs) < states)
    low2 = lax.rem(iota((2 * chs, LANES), 1) // (2 * chs), 2) == 0
    low1 = lax.rem(iota((chs, LANES), 1) // chs, 2) == 0

    for copy in small:
        copy.wait()
    seq = jnp.concatenate([v_jm[...]] * (rows // chs), axis=1)
    picker = jnp.where(same & (z_pick == seq), 1.0, 0.0)
    moved = lax.dot_general(
        v_fac[0], jnp.where(left_rows, picker, 0.0).astype(BF16), NT, preferred_element_type=F32
    ) + lax.dot_general(
        v_fac[1], jnp.where(left_rows, 0.0, picker).astype(BF16), NT, preferred_element_type=F32
    )
    gathered[0] = moved.astype(BF16)

    def swap_blocks(tile):
        a, b = tile[: 2 * chs], tile[2 * chs :]
        ab = (
            jnp.where(low2, a, pltpu.roll(b, 2 * chs, 1)),
            jnp.where(low2, pltpu.roll(a, LANES - 2 * chs, 1), b),
        )
        out = []
        for half in ab:
            a, b = half[:chs], half[chs:]
            out.append(jnp.where(low1, a, pltpu.roll(b, chs, 1)))
            out.append(jnp.where(low1, pltpu.roll(a, LANES - chs, 1), b))
        return jnp.concatenate(out, axis=0)

    def products(c):
        for h in range(2):
            right_in[h][c].wait()
        return [
            jnp.dot(v_left[h], v_right[h, :, pl.ds(c * chunk, chunk)], preferred_element_type=F32)
            for h in range(2)
        ]

    def finish(c, fulls):
        for h in range(2):
            for i in range(2):
                tile = jnp.where(live, fulls[h][:, i * LANES : (i + 1) * LANES], 0.0)
                outgoing[h, 2 * c + i] = swap_blocks(tile).astype(BF16)

    def half_copy(h, c):
        return pltpu.make_async_remote_copy(
            src_ref=outgoing.at[h, pl.ds(2 * c, 2)],
            dst_ref=incoming.at[pl.ds(2 * c, 2), pl.ds(h * rows, rows)],
            send_sem=h_send,
            recv_sem=h_recv.at[h, c],
            device_id={"sec": near[h]},
            device_id_type=MESH,
        )

    def row_copy(buffer, send_sem, recv_sem, offset):
        return pltpu.make_async_remote_copy(
            src_ref=buffer.at[0],
            dst_ref=buffer.at[n_row - offset],
            send_sem=send_sem,
            recv_sem=recv_sem,
            device_id={"row": peer(offset)},
            device_id_type=MESH,
        )

    def all_rows(buffer, send_sem, recv_sem):
        others = buffer.at[pl.ds(1, n_row - 1)]
        return pltpu.make_async_remote_copy(
            src_ref=others, dst_ref=others, send_sem=send_sem, recv_sem=recv_sem,
            device_id={"row": peer(1)}, device_id_type=MESH,
        )

    early = chunks // 2
    for h in range(2):
        left_in[h].wait()
    fulls = products(0)
    for c in range(1, early):
        following = products(c)
        finish(c - 1, fulls)
        fulls = following
    pl.semaphore_wait(barrier, n_row - 1 + 2)
    for offset in offsets:
        row_copy(gathered, g_send, g_recv, offset).start()
    for c in range(early - 1):
        for h in range(2):
            half_copy(h, c).start()
    for c in range(early, chunks + 1):
        following = products(c) if c < chunks else None
        finish(c - 1, fulls)
        for h in range(2):
            half_copy(h, c - 1).start()
        fulls = following

    w_row = jnp.where(iota((1, ks), 1) < kp[0], 1.0 / jnp.sqrt(v_sg[...]), 0.0)
    diagonal = iota((ks, ks), 0) == iota((ks, ks), 1)
    weight = jnp.sum(jnp.where(diagonal, jnp.broadcast_to(w_row, (ks, ks)), 0.0), axis=1, keepdims=True)

    all_rows(gathered, g_send, g_recv).wait_recv()
    upper_lanes = iota((2 * ks, LANES), 1) < rows
    zero = jnp.zeros((2 * ks, LANES), BF16)

    def factor(t):
        slots = [lax.rem(2 * t + g - row + n_row, n_row) for g in range(2)]
        both = jnp.concatenate([gathered[slot] for slot in slots], axis=0)
        return jnp.concatenate([jnp.where(upper_lanes, both, zero), jnp.where(upper_lanes, zero, both)], axis=0)

    total = jnp.zeros((4 * ks, LANES), F32)
    for c in range(chunks):
        lhs = jnp.concatenate([factor(2 * c), factor(2 * c + 1)], axis=1)
        for h in range(2):
            half_copy(h, c).wait_recv()
        rhs = incoming[pl.ds(2 * c, 2)].reshape(2 * LANES, LANES)
        total = total + jnp.dot(lhs, rhs, preferred_element_type=F32)
    scaled = [
        (total[2 * h * ks : (2 * h + 1) * ks, :rows] + total[(2 * h + 1) * ks : (2 * h + 2) * ks, rows:]) * weight
        for h in range(2)
    ]
    high = [v.astype(BF16) for v in scaled]
    low = [(v - u.astype(F32)).astype(BF16) for v, u in zip(scaled, high)]
    pt[...] = high[0]
    pj[...] = high[1]

    groups = LANES // ks
    wide = lax.dot_general(
        jnp.concatenate([high[0], low[0]], axis=0),
        jnp.concatenate([high[1]] * groups + [low[1]] * groups, axis=0),
        NT,
        preferred_element_type=F32,
    )
    wide = (wide[:ks, :LANES] + (wide[:ks, LANES:] + wide[ks:, :LANES])) + wide[ks:, LANES:]
    own = lax.rem(iota((ks, LANES), 0), groups) == iota((ks, LANES), 1) // ks
    wide = jnp.where(own, wide, 0.0)
    for i in range(ks // groups):
        partial[0, pl.ds(i, 1)] = jnp.sum(wide[i * groups : (i + 1) * groups], axis=0, keepdims=True)
    for offset in offsets:
        row_copy(partial, i_send, i_recv, offset).start()

    all_rows(gathered, g_send, g_recv).wait_send()
    pltpu.make_async_remote_copy(
        src_ref=outgoing, dst_ref=outgoing, send_sem=h_send, recv_sem=h_send,
        device_id={"sec": near[0]}, device_id_type=MESH,
    ).wait_send()
    all_rows(partial, i_send, i_recv).wait_recv()
    terms = [partial[i] for i in range(n_row)]
    while len(terms) > 1:
        terms = [a + b for a, b in zip(terms[::2], terms[1::2])]
    spread = jnp.concatenate(
        [jnp.broadcast_to(terms[0][i : i + 1], (groups, LANES)) for i in range(ks // groups)], axis=0
    )
    spread = jnp.where(own, spread, 0.0)
    shift = LANES // 2
    while shift >= ks:
        spread = spread + pltpu.roll(spread, shift, 1)
        shift //= 2
    it[...] = spread[:, :ks] / jnp.sqrt(F32(width))
    all_rows(partial, i_send, i_recv).wait_send()


def put_kernel(pt, pj, it, pt_out, pj_out, it_out, sem):
    copies = [
        pltpu.make_async_copy(a, b, sem.at[i])
        for i, (a, b) in enumerate(((pt, pt_out), (pj, pj_out), (it, it_out)))
    ]
    for copy in copies:
        copy.start()
    for copy in copies:
        copy.wait()


def local(
    corner_ul, corner_ur, corner_dl, corner_dr, left_factor, right_factor, singular, states, kept, joining_map
):
    n_sec, n_row = lax.axis_size("sec"), lax.axis_size("row")
    rows, width = corner_ul.shape[1:]
    ks = left_factor.shape[2]
    chs = joining_map.shape[1]
    tiles = width // LANES
    chunks = tiles // 2
    dma = pltpu.SemaphoreType.DMA
    hbm = pl.BlockSpec(memory_space=pltpu.HBM)
    smem = pl.BlockSpec(memory_space=pltpu.SMEM)
    vmem = pl.BlockSpec(memory_space=pltpu.VMEM)
    shapes = (((ks, rows), BF16), ((ks, rows), BF16), ((ks, ks), F32))
    results = pl.pallas_call(
        functools.partial(kernel, n_sec, n_row),
        out_shape=tuple(pltpu.VMEM(*s) for s in shapes),
        in_specs=[hbm] * 7 + [smem] * 2 + [hbm],
        out_specs=(vmem,) * 3,
        scratch_shapes=[
            pltpu.VMEM((2, rows, width), BF16),
            pltpu.VMEM((2, width, width), BF16),
            pltpu.VMEM((2, ks, rows), BF16),
            pltpu.VMEM((1, ks), F32),
            pltpu.VMEM((1, chs), jnp.int32),
            pltpu.VMEM((n_row, ks, 2 * rows), BF16),
            pltpu.VMEM((2, tiles, rows, LANES), BF16),
            pltpu.VMEM((tiles, 2 * rows, LANES), BF16),
            pltpu.VMEM((n_row, ks * ks // LANES, LANES), F32),
            dma((2, chunks)),
            dma((6,)),
            dma,
            dma,
            dma,
            dma((2, chunks)),
            dma,
            dma,
        ],
        compiler_params=pltpu.CompilerParams(collective_id=0, has_side_effects=True),
    )(
        corner_ul[0], corner_ur[0], corner_dl[0], corner_dr[0],
        left_factor[0].T, right_factor[0].T,
        singular, states, kept, joining_map,
    )
    pt, pj, it = pl.pallas_call(
        put_kernel,
        out_shape=tuple(jax.ShapeDtypeStruct(*s) for s in shapes),
        in_specs=[vmem] * 3,
        out_specs=(hbm,) * 3,
        scratch_shapes=[dma((3,))],
    )(*(pltpu.with_memory_space_constraint(v, pltpu.VMEM) for v in results))
    return pt.T[None], pj.T[None], it[None]


def solution(mesh):
    placed = (
        P("sec", "row", None),
        P("sec", None, None),
        P("sec", "row", None),
        P("sec", None, None),
        P("sec", "row", None),
        P("sec", "row", None),
        P("sec", None),
        P("sec"),
        P("sec"),
        P("sec", None),
    )
    return jax.shard_map(
        local,
        mesh=mesh,
        in_specs=placed,
        out_specs=(P("sec", "row", None), P("sec", "row", None), P("sec", None, None)),
        check_vma=False,
    )
```

time: 38.1 us -> 30.3 us (0.80)
  local copies, waits for them, and re-layouts: 3.83 us -> 0 us
  Pallas kernels: 32.1 us -> 28.3 us
    unnamed x3 -> x0, local copies, waits for them, and re-layouts: 3.83 us -> none
    pallas_call x1 -> x2, Pallas kernels: 32.1 us -> 28.3 us  [the longest x1 27.6 us: local(): pl.pallas_call(functools.partial(kernel, n_sec, n_row), out_shape=tuple((...]
where the time goes in v2:
time: 30.3 us; the launch traced here: 30.2 us
  Pallas kernels  28.3 us (93%)
  between operations  1.93 us (6%)
    pallas_call x1, Pallas kernels, local(): pl.pallas_call(functools.partial(kernel, n_sec, n_row), out_shape=tuple((...  27.6 us
    pallas_call x1, Pallas kernels, local(): pl.pallas_call(put_kernel, out_shape=tuple((jax.ShapeDtypeStruct(*s) for...  0.64 us

profile of v2, /device:TPU:1, one launch (start us, length us, event | category | flops | bytes accessed | tf_op | source)
XLA Modules:
  0.0 30.2 jit_solution(2676188265132482304)
XLA Ops:
  1.9 27.6 %shard_map.121 = (bf16[16,64]{1,0:T(8,128)(2,1)S(1)}, bf16[16,64]{1,0:T(8,128)(2,1)S(1)}, f32[16,16]{1,0:T(8,128)S(1)}) custom-call(bf16[64,1024]{1,0:T(8,128)(2,1)} %bitcast.19, bf16[1024,1024]{1,0:T(8,128)(2,1)} %bitcast.17, bf16[64,1024]{1,0:T(8,128)(2,1)} %bitcast.20, bf16[1024,1024]{1,0:T(8,128)(2,1)} %bitcast.18, bf16[16,64]{1,0:T(8,128)(2,1)} %bitcast.21, ...), custom_call_target="tpu_custom_call" | custom-call | tf_op jit(solution)/shard_map/pallas_call | solution.py:260
  29.6 0.6 %shard_map.122 = (bf16[16,64]{1,0:T(8,128)(2,1)}, bf16[16,64]{1,0:T(8,128)(2,1)}, f32[16,16]{1,0:T(8,128)}) custom-call(bf16[16,64]{1,0:T(8,128)(2,1)S(1)} %get-tuple-element.9.pt, bf16[16,64]{1,0:T(8,128)(2,1)S(1)} %get-tuple-element.10.pj, f32[16,16]{1,0:T(8,128)S(1)} %get-tuple-element.11.it), custom_call_target="tpu_custom_call" | custom-call | tf_op jit(solution)/shard_map/pallas_call | solution.py:290

commit v3 on v2

--- a/solution.py
+++ b/solution.py
@@ -14,19 +14,24 @@
 NT = (((1,), (1,)), ((), ()))
 
 
+def chunk_list(tiles):
+    sizes = [2] * (tiles // 2)
+    return [(sum(sizes[:i]), size) for i, size in enumerate(sizes)]
+
+
 def kernel(
     n_sec, n_row,
     ul, ur, dl, dr, lf, rf, sg, st, kp, jm,
     pt, pj, it,
     v_left, v_right, v_fac, v_sg, v_jm,
     gathered, outgoing, incoming, partial,
-    big_sem, small_sem, g_send, g_recv, h_send, h_recv, i_send, i_recv,
+    right_sem, left_sem, fac_sem, jm_sem, sg_sem, g_send, g_recv, h_send, h_recv, i_send, i_recv,
 ):
     rows, width = ul.shape
     ks = lf.shape[0]
     chs = jm.shape[1]
-    chunk = 2 * LANES
-    chunks = width // chunk
+    tiles = width // LANES
+    chunks = chunk_list(tiles)
     sec = lax.axis_index("sec")
     row = lax.axis_index("row")
     near = (lax.rem(sec + 1, n_sec), lax.rem(sec + n_sec - 1, n_sec))
@@ -35,38 +40,36 @@
     def peer(offset):
         return lax.rem(row + offset, n_row)
 
-    lefts, rights = (ul, dl), (ur, dr)
-    left_in = [pltpu.make_async_copy(lefts[h], v_left.at[h], small_sem.at[4 + h]) for h in range(2)]
-    right_in = [
-        [
-            pltpu.make_async_copy(
-                rights[h].at[:, pl.ds(c * chunk, chunk)],
-                v_right.at[h, :, pl.ds(c * chunk, chunk)],
-                big_sem.at[h, c],
-            )
-            for c in range(chunks)
-        ]
-        for h in range(2)
-    ]
-    small = [
-        pltpu.make_async_copy(lf, v_fac.at[0], small_sem.at[0]),
-        pltpu.make_async_copy(rf, v_fac.at[1], small_sem.at[1]),
-        pltpu.make_async_copy(jm, v_jm, small_sem.at[2]),
-        pltpu.make_async_copy(sg, v_sg, small_sem.at[3]),
-    ]
-    for copy in small:
-        copy.start()
-    for h in range(2):
-        left_in[h].start()
-    for c in range(chunks):
-        for h in range(2):
-            right_in[h][c].start()
-
+    lefts, rights, factors = (ul, dl), (ur, dr), (lf, rf)
+    rounds = [[(h, i - h) for h in range(2) if 0 <= i - h < len(chunks)] for i in range(len(chunks) + 1)]
+
+    def columns(c):
+        return pl.ds(chunks[c][0] * LANES, chunks[c][1] * LANES)
+
+    def left_in(h):
+        return pltpu.make_async_copy(lefts[h], v_left.at[h], left_sem.at[h])
+
+    def right_in(h, c):
+        return pltpu.make_async_copy(
+            rights[h].at[:, columns(c)], v_right.at[h, :, columns(c)], right_sem.at[h, c]
+        )
+
+    left_in(0).start()
+    right_in(0, 0).start()
     barrier = pltpu.get_barrier_semaphore()
+    for offset in offsets:
+        pl.semaphore_signal(barrier, inc=1, device_id={"row": peer(offset)}, device_id_type=MESH)
     for other in near:
         pl.semaphore_signal(barrier, inc=1, device_id={"sec": other}, device_id_type=MESH)
-    for offset in offsets:
-        pl.semaphore_signal(barrier, inc=1, device_id={"row": peer(offset)}, device_id_type=MESH)
+    left_in(1).start()
+    for h, c in rounds[1]:
+        right_in(h, c).start()
+    for h in range(2):
+        pltpu.make_async_copy(factors[h], v_fac.at[h], fac_sem).start()
+    jm_in = pltpu.make_async_copy(jm, v_jm, jm_sem)
+    sg_in = pltpu.make_async_copy(sg, v_sg, sg_sem)
+    jm_in.start()
+    sg_in.start()
 
     def iota(shape, axis):
         return lax.broadcasted_iota(jnp.int32, shape, axis)
@@ -81,17 +84,6 @@
     low2 = lax.rem(iota((2 * chs, LANES), 1) // (2 * chs), 2) == 0
     low1 = lax.rem(iota((chs, LANES), 1) // chs, 2) == 0
 
-    for copy in small:
-        copy.wait()
-    seq = jnp.concatenate([v_jm[...]] * (rows // chs), axis=1)
-    picker = jnp.where(same & (z_pick == seq), 1.0, 0.0)
-    moved = lax.dot_general(
-        v_fac[0], jnp.where(left_rows, picker, 0.0).astype(BF16), NT, preferred_element_type=F32
-    ) + lax.dot_general(
-        v_fac[1], jnp.where(left_rows, 0.0, picker).astype(BF16), NT, preferred_element_type=F32
-    )
-    gathered[0] = moved.astype(BF16)
-
     def swap_blocks(tile):
         a, b = tile[: 2 * chs], tile[2 * chs :]
         ab = (
@@ -105,24 +97,28 @@
             out.append(jnp.where(low1, pltpu.roll(a, LANES - chs, 1), b))
         return jnp.concatenate(out, axis=0)
 
-    def products(c):
-        for h in range(2):
-            right_in[h][c].wait()
-        return [
-            jnp.dot(v_left[h], v_right[h, :, pl.ds(c * chunk, chunk)], preferred_element_type=F32)
-            for h in range(2)
-        ]
-
-    def finish(c, fulls):
-        for h in range(2):
-            for i in range(2):
-                tile = jnp.where(live, fulls[h][:, i * LANES : (i + 1) * LANES], 0.0)
-                outgoing[h, 2 * c + i] = swap_blocks(tile).astype(BF16)
+    def own_factors():
+        seq = jnp.concatenate([v_jm[...]] * (rows // chs), axis=1)
+        picker = jnp.where(same & (z_pick == seq), 1.0, 0.0)
+        moved = lax.dot_general(
+            v_fac[0], jnp.where(left_rows, picker, 0.0).astype(BF16), NT, preferred_element_type=F32
+        ) + lax.dot_general(
+            v_fac[1], jnp.where(left_rows, 0.0, picker).astype(BF16), NT, preferred_element_type=F32
+        )
+        gathered[0] = moved.astype(BF16)
+
+    def product(h, c):
+        return jnp.dot(v_left[h], v_right[h, :, columns(c)], preferred_element_type=F32)
+
+    def finish(h, c, full):
+        for i in range(chunks[c][1]):
+            tile = jnp.where(live, full[:, i * LANES : (i + 1) * LANES], 0.0)
+            outgoing[h, chunks[c][0] + i] = swap_blocks(tile).astype(BF16)
 
     def half_copy(h, c):
         return pltpu.make_async_remote_copy(
-            src_ref=outgoing.at[h, pl.ds(2 * c, 2)],
-            dst_ref=incoming.at[pl.ds(2 * c, 2), pl.ds(h * rows, rows)],
+            src_ref=outgoing.at[h, pl.ds(*chunks[c])],
+            dst_ref=incoming.at[pl.ds(*chunks[c]), pl.ds(h * rows, rows)],
             send_sem=h_send,
             recv_sem=h_recv.at[h, c],
             device_id={"sec": near[h]},
@@ -146,27 +142,32 @@
             device_id={"row": peer(1)}, device_id_type=MESH,
         )
 
-    early = chunks // 2
-    for h in range(2):
-        left_in[h].wait()
-    fulls = products(0)
-    for c in range(1, early):
-        following = products(c)
-        finish(c - 1, fulls)
-        fulls = following
-    pl.semaphore_wait(barrier, n_row - 1 + 2)
-    for offset in offsets:
-        row_copy(gathered, g_send, g_recv, offset).start()
-    for c in range(early - 1):
-        for h in range(2):
+    for i, parts in enumerate(rounds):
+        if i < 2:
+            left_in(i).wait()
+        for h, c in parts:
+            right_in(h, c).wait()
+        if i == 0:
+            for later in rounds[2:]:
+                for h, c in later:
+                    right_in(h, c).start()
+        if i == 1:
+            pltpu.make_async_copy(v_fac, v_fac, fac_sem).wait()
+            jm_in.wait()
+        fulls = [product(h, c) for h, c in parts]
+        if i == 1:
+            own_factors()
+        for (h, c), full in zip(parts, fulls):
+            finish(h, c, full)
+        if i == 0:
+            pl.semaphore_wait(barrier, n_row - 1 + 2)
+        for h, c in parts:
             half_copy(h, c).start()
-    for c in range(early, chunks + 1):
-        following = products(c) if c < chunks else None
-        finish(c - 1, fulls)
-        for h in range(2):
-            half_copy(h, c - 1).start()
-        fulls = following
-
+        if i == 1:
+            for offset in offsets:
+                row_copy(gathered, g_send, g_recv, offset).start()
+
+    sg_in.wait()
     w_row = jnp.where(iota((1, ks), 1) < kp[0], 1.0 / jnp.sqrt(v_sg[...]), 0.0)
     diagonal = iota((ks, ks), 0) == iota((ks, ks), 1)
     weight = jnp.sum(jnp.where(diagonal, jnp.broadcast_to(w_row, (ks, ks)), 0.0), axis=1, keepdims=True)
@@ -181,11 +182,12 @@
         return jnp.concatenate([jnp.where(upper_lanes, both, zero), jnp.where(upper_lanes, zero, both)], axis=0)
 
     total = jnp.zeros((4 * ks, LANES), F32)
-    for c in range(chunks):
-        lhs = jnp.concatenate([factor(2 * c), factor(2 * c + 1)], axis=1)
-        for h in range(2):
-            half_copy(h, c).wait_recv()
-        rhs = incoming[pl.ds(2 * c, 2)].reshape(2 * LANES, LANES)
+    for c in range(len(chunks)):
+        half_copy(1, c).wait_recv()
+    for c, (first, count) in enumerate(chunks):
+        lhs = jnp.concatenate([factor(first + i) for i in range(count)], axis=1)
+        half_copy(0, c).wait_recv()
+        rhs = incoming[pl.ds(first, count)].reshape(count * LANES, LANES)
         total = total + jnp.dot(lhs, rhs, preferred_element_type=F32)
     scaled = [
         (total[2 * h * ks : (2 * h + 1) * ks, :rows] + total[(2 * h + 1) * ks : (2 * h + 2) * ks, rows:]) * weight
@@ -204,7 +206,7 @@
         preferred_element_type=F32,
     )
     wide = (wide[:ks, :LANES] + (wide[:ks, LANES:] + wide[ks:, :LANES])) + wide[ks:, LANES:]
-    own = lax.rem(iota((ks, LANES), 0), groups) == iota((ks, LANES), 1) // ks
+    own = lax.rem(iota((ks, LANES), 0) + iota((ks, LANES), 1) // ks, groups) == 0
     wide = jnp.where(own, wide, 0.0)
     for i in range(ks // groups):
         partial[0, pl.ds(i, 1)] = jnp.sum(wide[i * groups : (i + 1) * groups], axis=0, keepdims=True)
@@ -221,13 +223,12 @@
     while len(terms) > 1:
         terms = [a + b for a, b in zip(terms[::2], terms[1::2])]
     spread = jnp.concatenate(
-        [jnp.broadcast_to(terms[0][i : i + 1], (groups, LANES)) for i in range(ks // groups)], axis=0
-    )
-    spread = jnp.where(own, spread, 0.0)
-    shift = LANES // 2
-    while shift >= ks:
-        spread = spread + pltpu.roll(spread, shift, 1)
-        shift //= 2
+        [
+            pltpu.roll(jnp.broadcast_to(terms[0][i : i + 1], (groups, LANES)), 0, 1, stride=ks, stride_axis=0)
+            for i in range(ks // groups)
+        ],
+        axis=0,
+    )
     it[...] = spread[:, :ks] / jnp.sqrt(F32(width))
     all_rows(partial, i_send, i_recv).wait_send()
 
@@ -251,7 +252,7 @@
     ks = left_factor.shape[2]
     chs = joining_map.shape[1]
     tiles = width // LANES
-    chunks = tiles // 2
+    chunks = len(chunk_list(tiles))
     dma = pltpu.SemaphoreType.DMA
     hbm = pl.BlockSpec(memory_space=pltpu.HBM)
     smem = pl.BlockSpec(memory_space=pltpu.SMEM)
@@ -273,7 +274,10 @@
             pltpu.VMEM((tiles, 2 * rows, LANES), BF16),
             pltpu.VMEM((n_row, ks * ks // LANES, LANES), F32),
             dma((2, chunks)),
-            dma((6,)),
+            dma((2,)),
+            dma,
+            dma,
+            dma,
             dma,
             dma,
             dma,

time: 30.3 us -> 29.1 us (0.960)
  Pallas kernels: 28.3 us -> 27 us
    pallas_call x1, Pallas kernels: 27.6 us -> 26.4 us  [local(): pl.pallas_call(functools.partial(kernel, n_sec, n_row), out_shape=tuple((...]
where the time goes in v3:
time: 29.1 us; the launch traced here: 29 us
  Pallas kernels  27 us (93%)
  between operations  1.93 us (7%)
    pallas_call x1, Pallas kernels, local(): pl.pallas_call(functools.partial(kernel, n_sec, n_row), out_shape=tuple((...  26.4 us
    pallas_call x1, Pallas kernels, local(): pl.pallas_call(put_kernel, out_shape=tuple((jax.ShapeDtypeStruct(*s) for...  0.64 us

profile of v3, /device:TPU:1, one launch (start us, length us, event | category | flops | bytes accessed | tf_op | source)
XLA Modules:
  0.0 29.0 jit_solution(11491225980136736057)
XLA Ops:
  1.9 26.4 %shard_map.121 = (bf16[16,64]{1,0:T(8,128)(2,1)S(1)}, bf16[16,64]{1,0:T(8,128)(2,1)S(1)}, f32[16,16]{1,0:T(8,128)S(1)}) custom-call(bf16[64,1024]{1,0:T(8,128)(2,1)} %bitcast.19, bf16[1024,1024]{1,0:T(8,128)(2,1)} %bitcast.17, bf16[64,1024]{1,0:T(8,128)(2,1)} %bitcast.20, bf16[1024,1024]{1,0:T(8,128)(2,1)} %bitcast.18, bf16[16,64]{1,0:T(8,128)(2,1)} %bitcast.21, ...), custom_call_target="tpu_custom_call" | custom-call | tf_op jit(solution)/shard_map/pallas_call | solution.py:261
  28.3 0.6 %shard_map.122 = (bf16[16,64]{1,0:T(8,128)(2,1)}, bf16[16,64]{1,0:T(8,128)(2,1)}, f32[16,16]{1,0:T(8,128)}) custom-call(bf16[16,64]{1,0:T(8,128)(2,1)S(1)} %get-tuple-element.9.pt, bf16[16,64]{1,0:T(8,128)(2,1)S(1)} %get-tuple-element.10.pj, f32[16,16]{1,0:T(8,128)S(1)} %get-tuple-element.11.it), custom_call_target="tpu_custom_call" | custom-call | tf_op jit(solution)/shard_map/pallas_call | solution.py:294

commit v4 on v3

--- a/solution.py
+++ b/solution.py
@@ -49,10 +49,18 @@
     def left_in(h):
         return pltpu.make_async_copy(lefts[h], v_left.at[h], left_sem.at[h])
 
+    def held(h, tile, count):
+        return pl.ds((tile + 2 * h) * LANES, count * LANES)
+
     def right_in(h, c):
         return pltpu.make_async_copy(
-            rights[h].at[:, columns(c)], v_right.at[h, :, columns(c)], right_sem.at[h, c]
-        )
+            rights[h].at[:, columns(c)], v_right.at[h, :, held(h, *chunks[c])], right_sem.at[c + h]
+        )
+
+    def round_in(parts):
+        h, c = parts[0]
+        landed = v_right.at[pl.ds(h, len(parts)), :, held(h, *chunks[c])]
+        return pltpu.make_async_copy(landed, landed, right_sem.at[c + h])
 
     left_in(0).start()
     right_in(0, 0).start()
@@ -107,20 +115,41 @@
         )
         gathered[0] = moved.astype(BF16)
 
-    def product(h, c):
-        return jnp.dot(v_left[h], v_right[h, :, columns(c)], preferred_element_type=F32)
+    def product(h, c, alone):
+        if alone:
+            first, count = chunks[c]
+            return jnp.concatenate(
+                [
+                    jnp.dot(v_left[h], v_right[h, :, held(h, t, 1)], preferred_element_type=F32)
+                    for t in range(first, first + count)
+                ],
+                axis=1,
+            )
+        return jnp.dot(v_left[h], v_right[h, :, held(h, *chunks[c])], preferred_element_type=F32)
 
     def finish(h, c, full):
         for i in range(chunks[c][1]):
             tile = jnp.where(live, full[:, i * LANES : (i + 1) * LANES], 0.0)
             outgoing[h, chunks[c][0] + i] = swap_blocks(tile).astype(BF16)
+
+    last = len(chunks) - 1
+
+    def arrival(h, c):
+        return 0 if h else 1 + c // max(last, 1)
+
+    def wait_half(h, first, count):
+        landed = incoming.at[pl.ds(first, count), pl.ds(h * rows, rows)]
+        pltpu.make_async_remote_copy(
+            src_ref=landed, dst_ref=landed, send_sem=h_send, recv_sem=h_recv.at[arrival(h, first // 2)],
+            device_id={"sec": near[h]}, device_id_type=MESH,
+        ).wait_recv()
 
     def half_copy(h, c):
         return pltpu.make_async_remote_copy(
             src_ref=outgoing.at[h, pl.ds(*chunks[c])],
             dst_ref=incoming.at[pl.ds(*chunks[c]), pl.ds(h * rows, rows)],
             send_sem=h_send,
-            recv_sem=h_recv.at[h, c],
+            recv_sem=h_recv.at[arrival(h, c)],
             device_id={"sec": near[h]},
             device_id_type=MESH,
         )
@@ -145,8 +174,7 @@
     for i, parts in enumerate(rounds):
         if i < 2:
             left_in(i).wait()
-        for h, c in parts:
-            right_in(h, c).wait()
+        round_in(parts).wait()
         if i == 0:
             for later in rounds[2:]:
                 for h, c in later:
@@ -154,7 +182,7 @@
         if i == 1:
             pltpu.make_async_copy(v_fac, v_fac, fac_sem).wait()
             jm_in.wait()
-        fulls = [product(h, c) for h, c in parts]
+        fulls = [product(h, c, len(parts) == 1) for h, c in parts]
         if i == 1:
             own_factors()
         for (h, c), full in zip(parts, fulls):
@@ -174,38 +202,56 @@
 
     all_rows(gathered, g_send, g_recv).wait_recv()
     upper_lanes = iota((2 * ks, LANES), 1) < rows
-    zero = jnp.zeros((2 * ks, LANES), BF16)
-
-    def factor(t):
-        slots = [lax.rem(2 * t + g - row + n_row, n_row) for g in range(2)]
-        both = jnp.concatenate([gathered[slot] for slot in slots], axis=0)
-        return jnp.concatenate([jnp.where(upper_lanes, both, zero), jnp.where(upper_lanes, zero, both)], axis=0)
-
-    total = jnp.zeros((4 * ks, LANES), F32)
+
+    def pair(t):
+        a, b = (
+            jnp.concatenate(
+                [gathered[lax.rem(2 * i + g - row + n_row, n_row)].astype(F32) for g in range(2)], axis=0
+            )
+            for i in (t, t + 1)
+        )
+        return (
+            jnp.where(upper_lanes, a, pltpu.roll(b, rows, 1)).astype(BF16),
+            jnp.where(upper_lanes, pltpu.roll(a, rows, 1), b).astype(BF16),
+        )
+
+    pairs = [pair(first) for first, _ in chunks]
+
+    def contract(h, c, total):
+        first, count = chunks[c]
+        rhs = incoming[pl.ds(first, count), pl.ds(h * rows, rows)].reshape(count * rows, LANES)
+        return total + jnp.dot(pairs[c][h], rhs, preferred_element_type=F32)
+
+    def parted(total):
+        return jnp.where(upper_lanes[:ks], total[:ks], total[ks:]) * weight
+
+    def folded(value):
+        return value + pltpu.roll(value, rows, 1)
+
+    def split(value):
+        high = value.astype(BF16)
+        return high, (value - high.astype(F32)).astype(BF16)
+
+    totals = [jnp.zeros((2 * ks, LANES), F32)] * 2
+    wait_half(1, 0, tiles)
     for c in range(len(chunks)):
-        half_copy(1, c).wait_recv()
-    for c, (first, count) in enumerate(chunks):
-        lhs = jnp.concatenate([factor(first + i) for i in range(count)], axis=1)
-        half_copy(0, c).wait_recv()
-        rhs = incoming[pl.ds(first, count)].reshape(count * LANES, LANES)
-        total = total + jnp.dot(lhs, rhs, preferred_element_type=F32)
-    scaled = [
-        (total[2 * h * ks : (2 * h + 1) * ks, :rows] + total[(2 * h + 1) * ks : (2 * h + 2) * ks, rows:]) * weight
-        for h in range(2)
-    ]
-    high = [v.astype(BF16) for v in scaled]
-    low = [(v - u.astype(F32)).astype(BF16) for v, u in zip(scaled, high)]
-    pt[...] = high[0]
-    pj[...] = high[1]
-
+        totals[1] = contract(1, c, totals[1])
+    scaled_b = folded(parted(totals[1]))
+    pj[...] = scaled_b[:, :rows].astype(BF16)
     groups = LANES // ks
+    high_b, low_b = (jnp.concatenate([v] * groups, axis=0) for v in split(scaled_b))
+    rhs_b = jnp.concatenate([high_b, low_b, high_b], axis=1)
+    wait_half(0, 0, tiles - 2)
+    for c in range(len(chunks)):
+        if c == last:
+            wait_half(0, tiles - 2, 2)
+        totals[0] = contract(0, c, totals[0])
+    parted_a = parted(totals[0])
+
+    high_a, low_a = split(parted_a)
     wide = lax.dot_general(
-        jnp.concatenate([high[0], low[0]], axis=0),
-        jnp.concatenate([high[1]] * groups + [low[1]] * groups, axis=0),
-        NT,
-        preferred_element_type=F32,
-    )
-    wide = (wide[:ks, :LANES] + (wide[:ks, LANES:] + wide[ks:, :LANES])) + wide[ks:, LANES:]
+        jnp.concatenate([high_a, high_a, low_a], axis=1), rhs_b, NT, preferred_element_type=F32
+    )
     own = lax.rem(iota((ks, LANES), 0) + iota((ks, LANES), 1) // ks, groups) == 0
     wide = jnp.where(own, wide, 0.0)
     for i in range(ks // groups):
@@ -213,6 +259,7 @@
     for offset in offsets:
         row_copy(partial, i_send, i_recv, offset).start()
 
+    pt[...] = folded(parted_a)[:, :rows].astype(BF16)
     all_rows(gathered, g_send, g_recv).wait_send()
     pltpu.make_async_remote_copy(
         src_ref=outgoing, dst_ref=outgoing, send_sem=h_send, recv_sem=h_send,
@@ -265,7 +312,7 @@
         out_specs=(vmem,) * 3,
         scratch_shapes=[
             pltpu.VMEM((2, rows, width), BF16),
-            pltpu.VMEM((2, width, width), BF16),
+            pltpu.VMEM((2, width, width + 2 * LANES), BF16),
             pltpu.VMEM((2, ks, rows), BF16),
             pltpu.VMEM((1, ks), F32),
             pltpu.VMEM((1, chs), jnp.int32),
@@ -273,7 +320,7 @@
             pltpu.VMEM((2, tiles, rows, LANES), BF16),
             pltpu.VMEM((tiles, 2 * rows, LANES), BF16),
             pltpu.VMEM((n_row, ks * ks // LANES, LANES), F32),
-            dma((2, chunks)),
+            dma((chunks + 1,)),
             dma((2,)),
             dma,
             dma,
@@ -281,7 +328,7 @@
             dma,
             dma,
             dma,
-            dma((2, chunks)),
+            dma((3,)),
             dma,
             dma,
         ],

time: 29.1 us -> 28.9 us (level)
  no operation moved by 1% of the time
where the time goes in v4:
time: 28.9 us; the launch traced here: 28.8 us
  Pallas kernels  26.8 us (93%)
  between operations  1.93 us (7%)
    pallas_call x1, Pallas kernels, local(): pl.pallas_call(functools.partial(kernel, n_sec, n_row), out_shape=tuple((...  26.2 us
    pallas_call x1, Pallas kernels, local(): pl.pallas_call(put_kernel, out_shape=tuple((jax.ShapeDtypeStruct(*s) for...  0.64 us

profile of v4, /device:TPU:1, one launch (start us, length us, event | category | flops | bytes accessed | tf_op | source)
XLA Modules:
  0.0 28.8 jit_solution(3922784789751879038)
XLA Ops:
  1.9 26.2 %shard_map.121 = (bf16[16,64]{1,0:T(8,128)(2,1)S(1)}, bf16[16,64]{1,0:T(8,128)(2,1)S(1)}, f32[16,16]{1,0:T(8,128)S(1)}) custom-call(bf16[64,1024]{1,0:T(8,128)(2,1)} %bitcast.19, bf16[1024,1024]{1,0:T(8,128)(2,1)} %bitcast.17, bf16[64,1024]{1,0:T(8,128)(2,1)} %bitcast.20, bf16[1024,1024]{1,0:T(8,128)(2,1)} %bitcast.18, bf16[16,64]{1,0:T(8,128)(2,1)} %bitcast.21, ...), custom_call_target="tpu_custom_call" | custom-call | tf_op jit(solution)/shard_map/pallas_call | solution.py:308
  28.1 0.6 %shard_map.122 = (bf16[16,64]{1,0:T(8,128)(2,1)}, bf16[16,64]{1,0:T(8,128)(2,1)}, f32[16,16]{1,0:T(8,128)}) custom-call(bf16[16,64]{1,0:T(8,128)(2,1)S(1)} %get-tuple-element.9.pt, bf16[16,64]{1,0:T(8,128)(2,1)S(1)} %get-tuple-element.10.pj, f32[16,16]{1,0:T(8,128)S(1)} %get-tuple-element.11.it), custom_call_target="tpu_custom_call" | custom-call | tf_op jit(solution)/shard_map/pallas_call | solution.py:341

commit v5 on v4

--- a/solution.py
+++ b/solution.py
@@ -240,7 +240,7 @@
     pj[...] = scaled_b[:, :rows].astype(BF16)
     groups = LANES // ks
     high_b, low_b = (jnp.concatenate([v] * groups, axis=0) for v in split(scaled_b))
-    rhs_b = jnp.concatenate([high_b, low_b, high_b], axis=1)
+    rhs_b = jnp.concatenate([high_b, low_b, high_b, low_b], axis=1)
     wait_half(0, 0, tiles - 2)
     for c in range(len(chunks)):
         if c == last:
@@ -250,7 +250,7 @@
 
     high_a, low_a = split(parted_a)
     wide = lax.dot_general(
-        jnp.concatenate([high_a, high_a, low_a], axis=1), rhs_b, NT, preferred_element_type=F32
+        jnp.concatenate([high_a, high_a, low_a, low_a], axis=1), rhs_b, NT, preferred_element_type=F32
     )
     own = lax.rem(iota((ks, LANES), 0) + iota((ks, LANES), 1) // ks, groups) == 0
     wide = jnp.where(own, wide, 0.0)

time: 28.9 us -> 28.9 us (level)
  no operation moved by 1% of the time
where the time goes in v5:
time: 28.9 us; the launch traced here: 28.8 us
  Pallas kernels  26.8 us (93%)
  between operations  1.93 us (7%)
    pallas_call x1, Pallas kernels, local(): pl.pallas_call(functools.partial(kernel, n_sec, n_row), out_shape=tuple((...  26.2 us
    pallas_call x1, Pallas kernels, local(): pl.pallas_call(put_kernel, out_shape=tuple((jax.ShapeDtypeStruct(*s) for...  0.64 us

profile of v5, /device:TPU:1, one launch (start us, length us, event | category | flops | bytes accessed | tf_op | source)
XLA Modules:
  0.0 28.8 jit_solution(9134348538770455020)
XLA Ops:
  1.9 26.2 %shard_map.121 = (bf16[16,64]{1,0:T(8,128)(2,1)S(1)}, bf16[16,64]{1,0:T(8,128)(2,1)S(1)}, f32[16,16]{1,0:T(8,128)S(1)}) custom-call(bf16[64,1024]{1,0:T(8,128)(2,1)} %bitcast.19, bf16[1024,1024]{1,0:T(8,128)(2,1)} %bitcast.17, bf16[64,1024]{1,0:T(8,128)(2,1)} %bitcast.20, bf16[1024,1024]{1,0:T(8,128)(2,1)} %bitcast.18, bf16[16,64]{1,0:T(8,128)(2,1)} %bitcast.21, ...), custom_call_target="tpu_custom_call" | custom-call | tf_op jit(solution)/shard_map/pallas_call | solution.py:308
  28.1 0.6 %shard_map.122 = (bf16[16,64]{1,0:T(8,128)(2,1)}, bf16[16,64]{1,0:T(8,128)(2,1)}, f32[16,16]{1,0:T(8,128)}) custom-call(bf16[16,64]{1,0:T(8,128)(2,1)S(1)} %get-tuple-element.9.pt, bf16[16,64]{1,0:T(8,128)(2,1)S(1)} %get-tuple-element.10.pj, f32[16,16]{1,0:T(8,128)S(1)} %get-tuple-element.11.it), custom_call_target="tpu_custom_call" | custom-call | tf_op jit(solution)/shard_map/pallas_call | solution.py:341

commit v6 on v5

--- a/solution.py
+++ b/solution.py
@@ -70,7 +70,7 @@
     for other in near:
         pl.semaphore_signal(barrier, inc=1, device_id={"sec": other}, device_id_type=MESH)
     left_in(1).start()
-    for h, c in rounds[1]:
+    for h, c in rounds[1] + rounds[2]:
         right_in(h, c).start()
     for h in range(2):
         pltpu.make_async_copy(factors[h], v_fac.at[h], fac_sem).start()
@@ -176,7 +176,7 @@
             left_in(i).wait()
         round_in(parts).wait()
         if i == 0:
-            for later in rounds[2:]:
+            for later in rounds[3:]:
                 for h, c in later:
                     right_in(h, c).start()
         if i == 1:

time: 28.9 us -> 28.9 us (level)
  no operation moved by 1% of the time
where the time goes in v6:
time: 28.9 us; the launch traced here: 28.8 us
  Pallas kernels  26.8 us (93%)
  between operations  1.93 us (7%)
    pallas_call x1, Pallas kernels, local(): pl.pallas_call(functools.partial(kernel, n_sec, n_row), out_shape=tuple((...  26.2 us
    pallas_call x1, Pallas kernels, local(): pl.pallas_call(put_kernel, out_shape=tuple((jax.ShapeDtypeStruct(*s) for...  0.64 us

profile of v6, /device:TPU:1, one launch (start us, length us, event | category | flops | bytes accessed | tf_op | source)
XLA Modules:
  0.0 28.8 jit_solution(1679741406927199939)
XLA Ops:
  1.9 26.2 %shard_map.121 = (bf16[16,64]{1,0:T(8,128)(2,1)S(1)}, bf16[16,64]{1,0:T(8,128)(2,1)S(1)}, f32[16,16]{1,0:T(8,128)S(1)}) custom-call(bf16[64,1024]{1,0:T(8,128)(2,1)} %bitcast.19, bf16[1024,1024]{1,0:T(8,128)(2,1)} %bitcast.17, bf16[64,1024]{1,0:T(8,128)(2,1)} %bitcast.20, bf16[1024,1024]{1,0:T(8,128)(2,1)} %bitcast.18, bf16[16,64]{1,0:T(8,128)(2,1)} %bitcast.21, ...), custom_call_target="tpu_custom_call" | custom-call | tf_op jit(solution)/shard_map/pallas_call | solution.py:308
  28.1 0.6 %shard_map.122 = (bf16[16,64]{1,0:T(8,128)(2,1)}, bf16[16,64]{1,0:T(8,128)(2,1)}, f32[16,16]{1,0:T(8,128)}) custom-call(bf16[16,64]{1,0:T(8,128)(2,1)S(1)} %get-tuple-element.9.pt, bf16[16,64]{1,0:T(8,128)(2,1)S(1)} %get-tuple-element.10.pj, f32[16,16]{1,0:T(8,128)S(1)} %get-tuple-element.11.it), custom_call_target="tpu_custom_call" | custom-call | tf_op jit(solution)/shard_map/pallas_call | solution.py:341
